TPU v7x, 512 devices: a whole 4x4x16 slice. The times are simulated.
512 devices in a mesh: dp: 16 (over z), segment: 2 (over y_hi), tensor: 16 (over x, y_lo, core).
Axes of the slice: x: 4, y: 4 (y_hi: 2, y_lo: 2; y = y_hi * 2 + y_lo), z: 16, core: 2. Of those that a mesh axis runs over, the one named last changes fastest.
Arguments:
- context: bfloat16 [1152, 4096], P(None, 'tensor'), may hold values from -6 to 6
- residual: bfloat16 [1152, 4096], P(None, 'dp'), may hold values from -6 to 6
- inverse_rms: float32 [1152], replicated, may hold values from 0.5 to 2
- norm_gain: float32 [4096], P('dp'), may hold values from 0.5 to 1.5
- gate_preact: bfloat16 [1152, 14336], P(None, 'tensor'), may hold values from -6 to 6
- up_preact: bfloat16 [1152, 14336], P(None, 'tensor'), may hold values from -6 to 6
- upstream: bfloat16 [1152, 4096], P(None, 'dp'), may hold values from -6 to 6
- gate_weight: bfloat16 [4096, 14336], P('dp', 'tensor'), may hold values from -0.09375 to 0.09375
- up_weight: bfloat16 [4096, 14336], P('dp', 'tensor'), may hold values from -0.09375 to 0.09375
- down_weight: bfloat16 [14336, 4096], P('tensor', 'dp'), may hold values from -0.046875 to 0.046875
- policy_logprob: float32 [32], replicated, may hold values from -270 to -230
- ref_logprob: float32 [32], replicated, may hold values from -270 to -230
- lengths: int32 [32], replicated, may hold values from 4061 to 4096
Outputs:
- residual_grad: bfloat16 [1152, 4096], P('tensor', 'dp')
- output_weight_grad: bfloat16 [4096, 4096], P('tensor', ('dp', 'segment'))
- gate_weight_grad: bfloat16 [4096, 14336], P(('dp', 'segment'), 'tensor')
- up_weight_grad: bfloat16 [4096, 14336], P(('dp', 'segment'), 'tensor')
- down_weight_grad: bfloat16 [14336, 4096], P('tensor', ('dp', 'segment'))
Inputs may be any that keep to these rules, and one draw needn't show every extreme that they name: `lengths`: the window holds positions 4060 to 4095 of every sequence; a position counts where it is below the sequence's length.
All inputs are finite; a program needn't handle non-finite values.
Results may differ from a plain program's by a relative error of at most 0.03.
Values may be sent and summed in bfloat16 or wider, within the bound.
A program may use at most 64 MiB of HBM per device.

v0:
```python
import jax
import jax.numpy as jnp
from jax import lax
from jax.sharding import PartitionSpec as P

D = 4096
POS = 36
LEN = 4096


def shifted(value, axis, steps):
    count = lax.axis_size(axis)
    first, last = (max(0, -steps), min(count, count - steps))
    return lax.ppermute(value, axis, [(source, source + steps) for source in range(first, last)])


def from_partner(value, axis, apart):
    mask = 2**apart
    pairs = [(source, source ^ mask) for source in range(lax.axis_size(axis))]
    return lax.ppermute(value, axis, pairs)


def token_weights(policy_logprob, ref_logprob, lengths, total_rows):
    npo_weight = 2.0 * jax.nn.sigmoid(0.1 * (policy_logprob - ref_logprob))
    positions = jnp.arange(total_rows, dtype=jnp.int32)
    sequence_of = positions // POS
    position_in = LEN - POS + positions % POS
    member = sequence_of[:, None] == jnp.arange(policy_logprob.shape[0], dtype=jnp.int32)[None, :]
    weight = jnp.sum(jnp.where(member, npo_weight[None, :], 0.0), axis=1)
    length_of = jnp.sum(jnp.where(member, lengths[None, :], 0), axis=1)
    return jnp.where(position_in < length_of, weight, 0.0)


def gate_grads_of(hidden_delta, gate_value, up_value):
    squash = jax.nn.sigmoid(gate_value)
    gate_delta = (hidden_delta * up_value * squash * (1.0 + gate_value * (1.0 - squash))).astype(
        jnp.bfloat16
    )
    up_delta = (hidden_delta * gate_value * squash).astype(jnp.bfloat16)
    return (gate_delta, up_delta)


def row_statistic(partial_dot):
    return lax.psum(partial_dot, "dp")


def finish_rows(weighted, residual, inverse_rms, norm_gain, normed_delta):
    residual_value = residual.astype(jnp.float32)
    row_dot = row_statistic(jnp.sum(norm_gain[None, :] * normed_delta * residual_value, axis=1))
    row_scale = inverse_rms * inverse_rms * inverse_rms * row_dot / D
    combined = (
        weighted.astype(jnp.float32)
        + inverse_rms[:, None] * norm_gain[None, :] * normed_delta
        - residual_value * row_scale[:, None]
    )
    return combined.astype(jnp.bfloat16)


def shards(
    context,
    residual,
    inverse_rms,
    norm_gain,
    gate_preact,
    up_preact,
    upstream,
    gate_weight,
    up_weight,
    down_weight,
    policy_logprob,
    ref_logprob,
    lengths,
):
    ffn_side = lax.axis_index("segment") == 1
    total_rows = residual.shape[0]
    features = residual.shape[1]
    hidden_width = gate_preact.shape[1]
    half_width = features // 2
    share_rows = total_rows // lax.axis_size("tensor")
    share_start = lax.axis_index("tensor") * share_rows
    token_weight = token_weights(policy_logprob, ref_logprob, lengths, total_rows)
    weighted = (upstream.astype(jnp.float32) * token_weight[:, None]).astype(jnp.bfloat16)
    normed = (residual.astype(jnp.float32) * inverse_rms[:, None] * norm_gain[None, :]).astype(
        jnp.bfloat16
    )
    gate_value = gate_preact.astype(jnp.float32)
    up_value = up_preact.astype(jnp.float32)
    hidden = (gate_value * jax.nn.sigmoid(gate_value) * up_value).astype(jnp.bfloat16)

    def down_part():
        return jnp.einsum("tf,td->fd", hidden, weighted, preferred_element_type=jnp.float32)

    down_full = lax.cond(
        ffn_side, down_part, lambda: jnp.zeros((hidden_width, features), jnp.float32)
    )
    hidden_delta = lax.psum(
        lax.cond(
            ffn_side,
            lambda: jnp.einsum(
                "td,fd->tf", weighted, down_weight, preferred_element_type=jnp.float32
            ),
            lambda: jnp.zeros((total_rows, hidden_width), jnp.float32),
        ).astype(jnp.bfloat16),
        "dp",
    ).astype(jnp.float32)
    gate_delta, up_delta = gate_grads_of(hidden_delta, gate_value, up_value)

    def weight_parts():
        gate_full = jnp.einsum("td,tf->df", normed, gate_delta, preferred_element_type=jnp.float32)
        up_full = jnp.einsum("td,tf->df", normed, up_delta, preferred_element_type=jnp.float32)
        return (gate_full, up_full)

    empty_grad = jnp.zeros((features, hidden_width), jnp.float32)
    gate_full, up_full = lax.cond(ffn_side, weight_parts, lambda: (empty_grad, empty_grad))

    def product():
        first_term = jnp.einsum(
            "tf,df->td", gate_delta, gate_weight, preferred_element_type=jnp.float32
        )
        return first_term + jnp.einsum(
            "tf,df->td", up_delta, up_weight, preferred_element_type=jnp.float32
        )

    normed_delta = lax.psum(
        lax.cond(ffn_side, product, lambda: jnp.zeros((total_rows, features), jnp.float32)).astype(
            jnp.bfloat16
        ),
        "tensor",
    ).astype(jnp.float32)
    grad_every = finish_rows(weighted, residual, inverse_rms, norm_gain, normed_delta)
    arrived = shifted(grad_every, "segment", -1)
    grad_tokens = jnp.where(ffn_side, grad_every, arrived)
    residual_grad = lax.dynamic_slice_in_dim(grad_tokens, share_start, share_rows, 0)

    def projection_part():
        return jnp.einsum("tc,td->cd", context, grad_tokens, preferred_element_type=jnp.float32)

    projection_full = lax.cond(
        ffn_side, lambda: jnp.zeros((context.shape[1], features), jnp.float32), projection_part
    )
    projection_bf = projection_full.astype(jnp.bfloat16)
    gate_bf = gate_full.astype(jnp.bfloat16)
    up_bf = up_full.astype(jnp.bfloat16)
    down_bf = down_full.astype(jnp.bfloat16)
    got_projection, got_gate, got_up, got_down = from_partner(
        (
            projection_bf[:, half_width:],
            gate_bf[:half_width],
            up_bf[:half_width],
            down_bf[:, :half_width],
        ),
        "segment",
        0,
    )
    output_weight_grad = jnp.where(ffn_side, got_projection, projection_bf[:, :half_width])
    gate_weight_grad = jnp.where(ffn_side, gate_bf[half_width:], got_gate)
    up_weight_grad = jnp.where(ffn_side, up_bf[half_width:], got_up)
    down_weight_grad = jnp.where(ffn_side, down_bf[:, half_width:], got_down)
    return (residual_grad, output_weight_grad, gate_weight_grad, up_weight_grad, down_weight_grad)


def solution(mesh):
    return jax.shard_map(
        shards,
        mesh=mesh,
        in_specs=(
            P(None, "tensor"),
            P(None, "dp"),
            P(),
            P("dp"),
            P(None, "tensor"),
            P(None, "tensor"),
            P(None, "dp"),
            P("dp", "tensor"),
            P("dp", "tensor"),
            P("tensor", "dp"),
            P(),
            P(),
            P(),
        ),
        out_specs=(
            P("tensor", "dp"),
            P("tensor", ("dp", "segment")),
            P(("dp", "segment"), "tensor"),
            P(("dp", "segment"), "tensor"),
            P("tensor", ("dp", "segment")),
        ),
        check_vma=False,
    )
```

profile of v0, /device:TPU:14, one launch (start us, length us, event | category | flops | bytes accessed | tf_op | source)
XLA Modules:
  0.0 375.4 jit_solution(5367766257168562192)
XLA Ops:
  7.2 0.7 divide_multiply_fusion
  7.9 0.1 select_reduce_fusion
  8.0 0.8 select_reduce_fusion.1
  8.8 1.3 multiply_convert_fusion
  10.1 0.2 conditional.5
  10.1 0.2 broadcast.64
  10.3 1.3 copy-done.2
  11.7 150.1 %all-reduce.3.cloned.1.call-done = bf16[1152,896]{1,0:T(8,128)(2,1)} async-done(((bf16[1152,896]{1,0:T(8,128)(2,1)}), bf16[1152,896]{1,0:T(8,128)(2,1)}) %all-reduce.3.cloned.1.call-update) | async-done | bytes 2064400 | tf_op jit(solution)/shard_map/psum | solution.py:96
  161.8 5.8 %fusion.3 = (bf16[1152,896]{1,0:T(8,128)(2,1)}, bf16[1152,896]{1,0:T(8,128)(2,1)S(1)}, bf16[1152,896]{1,0:T(8,128)(2,1)}) fusion(bf16[1152,896]{1,0:T(8,128)(2,1)} %param.28, bf16[1152,896]{1,0:T(8,128)(2,1)} %param.27, bf16[1152,896]{1,0:T(8,128)(2,1)} %all-reduce.3.cloned.1.call-done), kind=kLoop, calls=%fused_computation.10 | loop fusion | flops 19611648 | bytes 12386304 | tf_op jit(solution)/shard_map/convert_element_type | solution.py:88
  167.6 0.8 copy-done.3
  168.5 0.8 conditional.9
  168.5 0.8 broadcast.67
  169.3 1.0 slice.39
  170.3 9.2 %collective-permute-start.4 = (bf16[896,128]{1,0:T(8,128)(2,1)S(1)}, bf16[896,128]{1,0:T(8,128)(2,1)}, u32[]{:S(2)}, u32[]{:S(2)}) collective-permute-start(bf16[896,128]{1,0:T(8,128)(2,1)S(1)} %slice.39), channel_id=1, source_target_pairs={{0,16},{16,0},{1,17},{17,1},{2,18},{18,2},{3,19},{19,3},{4,20},{20... | collective-permute-start | bytes 688136 | tf_op jit(solution)/shard_map/ppermute | solution.py:20
  179.5 118.6 %all-reduce.5.cloned.1.call-done = bf16[1152,256]{1,0:T(8,128)(2,1)} async-done(((bf16[1152,256]{1,0:T(8,128)(2,1)}), bf16[1152,256]{1,0:T(8,128)(2,1)}) %all-reduce.5.cloned.1.call-update) | async-done | bytes 589840 | tf_op jit(solution)/shard_map/psum | solution.py:124
  298.1 1.3 fusion.13
  299.4 30.8 %psum.23 = f32[1152]{0:T(1024)S(1)} all-reduce(f32[1152]{0:T(1024)S(1)} %fusion.13), channel_id=1, replica_groups=mesh['dp'=16,'segment'=2,'tensor'=16] {'dp'}, use_global_device_ids=true, to_apply=%region_9.10 | all-reduce | flops 1152 | bytes 9216 | tf_op jit(solution)/shard_map/psum | solution.py:44
  330.3 2.7 fusion.15
  333.0 0.1 conditional.8
  333.1 5.9 %collective-permute-start.3 = (bf16[128,896]{1,0:T(8,128)(2,1)S(1)}, bf16[128,896]{1,0:T(8,128)(2,1)S(1)}, u32[]{:S(2)}, u32[]{:S(2)}) collective-permute-start(bf16[128,896]{1,0:T(8,128)(2,1)S(1)} %slice.37), channel_id=1, source_target_pairs={{0,16},{16,0},{1,17},{17,1},{2,18},{18,2},{3,19},{19,3},{4,20},{20... | collective-permute-start | bytes 688136 | tf_op jit(solution)/shard_map/ppermute | solution.py:20
  339.1 1.4 collective-permute-start
  340.5 1.8 slice_select_fusion
  342.3 6.0 %collective-permute-start.2 = (bf16[128,896]{1,0:T(8,128)(2,1)S(1)}, bf16[128,896]{1,0:T(8,128)(2,1)S(1)}, u32[]{:S(2)}, u32[]{:S(2)}) collective-permute-start(bf16[128,896]{1,0:T(8,128)(2,1)S(1)} %slice.35), channel_id=1, source_target_pairs={{0,16},{16,0},{1,17},{17,1},{2,18},{18,2},{3,19},{19,3},{4,20},{20... | collective-permute-start | bytes 688136 | tf_op jit(solution)/shard_map/ppermute | solution.py:20
  348.3 0.7 slice_select_fusion.1
  349.0 10.0 %collective-permute-done.2 = bf16[128,896]{1,0:T(8,128)(2,1)S(1)} collective-permute-done((bf16[128,896]{1,0:T(8,128)(2,1)S(1)}, bf16[128,896]{1,0:T(8,128)(2,1)S(1)}, u32[]{:S(2)}, u32[]{:S(2)}) %collective-permute-start.2) | collective-permute-done | bytes 229408 | tf_op jit(solution)/shard_map/ppermute | solution.py:20
  359.0 0.7 slice_select_fusion.2
  359.8 0.4 conditional.7
  359.8 0.4 fusion.27
  360.2 1.9 collective-permute-start.1
  362.1 0.6 constant_dynamic-slice_fusion
  362.8 5.1 %collective-permute-done.1 = bf16[256,128]{1,0:T(8,128)(2,1)S(1)} collective-permute-done((bf16[256,128]{1,0:T(8,128)(2,1)S(1)}, bf16[256,128]{1,0:T(8,128)(2,1)S(1)}, u32[]{:S(2)}, u32[]{:S(2)}) %collective-permute-start.1) | collective-permute-done | bytes 65568 | tf_op jit(solution)/shard_map/ppermute | solution.py:20
  367.9 0.6 slice_select_fusion.3
  (34 shorter events, 0.5 us)
Async XLA Ops:
  7.2 154.6 %all-reduce.3.cloned.1.call-start = ((), (), s32[]{:S(2)}) async-start(), calls=%async_computation | async-start | bytes 4128768 | tf_op jit(solution)/shard_map/psum | solution.py:96
  10.3 1.3 copy-start.2
  11.6 286.5 %all-reduce.5.cloned.1.call-start = ((), (), s32[]{:S(2)}) async-start(), calls=%async_computation.1 | async-start | bytes 1179648 | tf_op jit(solution)/shard_map/psum | solution.py:124
  167.6 0.8 copy-start.3
  168.4 129.7 %copy-start.5 = (bf16[1152,256]{1,0:T(8,128)(2,1)S(1)}, bf16[1152,256]{1,0:T(8,128)(2,1)}, u32[]{:S(2)}) copy-start(bf16[1152,256]{1,0:T(8,128)(2,1)} %param.24) | copy-start | bytes 1769476
  168.4 129.7 %copy-start.9 = (f32[256]{0:T(256)S(1)}, f32[256]{0:T(256)}, u32[]{:S(2)}) copy-start(f32[256]{0:T(256)} %param.26) | copy-start | bytes 3076
  168.4 161.8 %copy-start.8 = (f32[1152]{0:T(1024)S(1)}, f32[1152]{0:T(1024)}, u32[]{:S(2)}) copy-start(f32[1152]{0:T(1024)} %param.25) | copy-start | bytes 13828
  169.3 161.0 %copy-start.4 = (bf16[1152,256]{1,0:T(8,128)(2,1)S(1)}, bf16[1152,256]{1,0:T(8,128)(2,1)}, u32[]{:S(2)}) copy-start(bf16[1152,256]{1,0:T(8,128)(2,1)} %param.29) | copy-start | bytes 1769476
  170.3 170.2 %collective-permute-start.4 = (bf16[896,128]{1,0:T(8,128)(2,1)S(1)}, bf16[896,128]{1,0:T(8,128)(2,1)}, u32[]{:S(2)}, u32[]{:S(2)}) collective-permute-start(bf16[896,128]{1,0:T(8,128)(2,1)S(1)} %slice.39), channel_id=1, source_target_pairs={{0,16},{16,0},{1,17},{17,1},{2,18},{18,2},{3,19},{19,3},{4,20},{20... | collective-permute-start | bytes 688136 | tf_op jit(solution)/shard_map/ppermute | solution.py:20
  330.2 2.7 copy-start
  333.0 6.1 %copy-start.6 = (bf16[1152,256]{1,0:T(8,128)(2,1)S(1)}, bf16[1152,256]{1,0:T(8,128)(2,1)}, u32[]{:S(2)}) copy-start(bf16[1152,256]{1,0:T(8,128)(2,1)} %get-tuple-element.72) | copy-start | bytes 1769476
  333.1 15.2 %collective-permute-start.3 = (bf16[128,896]{1,0:T(8,128)(2,1)S(1)}, bf16[128,896]{1,0:T(8,128)(2,1)S(1)}, u32[]{:S(2)}, u32[]{:S(2)}) collective-permute-start(bf16[128,896]{1,0:T(8,128)(2,1)S(1)} %slice.37), channel_id=1, source_target_pairs={{0,16},{16,0},{1,17},{17,1},{2,18},{18,2},{3,19},{19,3},{4,20},{20... | collective-permute-start | bytes 688136 | tf_op jit(solution)/shard_map/ppermute | solution.py:20
  339.1 20.7 %copy-start.10 = (bf16[1152,256]{1,0:T(8,128)(2,1)S(1)}, bf16[1152,256]{1,0:T(8,128)(2,1)}, u32[]{:S(2)}) copy-start(bf16[1152,256]{1,0:T(8,128)(2,1)} %param.23) | copy-start | bytes 1769476
  339.1 20.7 %collective-permute-start = (bf16[1152,256]{1,0:T(8,128)(2,1)S(1)}, bf16[1152,256]{1,0:T(8,128)(2,1)S(1)}, u32[]{:S(2)}, u32[]{:S(2)}) collective-permute-start(bf16[1152,256]{1,0:T(8,128)(2,1)S(1)} %copy-done.6), channel_id=1, source_target_pairs={{16,0},{17,1},{18,2},{19,3},{20,4},{21,5},{22,6},{23,7},{24,8},{25... | collective-permute-start | bytes 1769480 | tf_op jit(solution)/shard_map/ppermute | solution.py:14
  342.3 16.7 %collective-permute-start.2 = (bf16[128,896]{1,0:T(8,128)(2,1)S(1)}, bf16[128,896]{1,0:T(8,128)(2,1)S(1)}, u32[]{:S(2)}, u32[]{:S(2)}) collective-permute-start(bf16[128,896]{1,0:T(8,128)(2,1)S(1)} %slice.35), channel_id=1, source_target_pairs={{0,16},{16,0},{1,17},{17,1},{2,18},{18,2},{3,19},{19,3},{4,20},{20... | collective-permute-start | bytes 688136 | tf_op jit(solution)/shard_map/ppermute | solution.py:20
  360.2 7.7 %collective-permute-start.1 = (bf16[256,128]{1,0:T(8,128)(2,1)S(1)}, bf16[256,128]{1,0:T(8,128)(2,1)S(1)}, u32[]{:S(2)}, u32[]{:S(2)}) collective-permute-start(bf16[256,128]{1,0:T(8,128)(2,1)S(1)} %slice.32), channel_id=1, source_target_pairs={{0,16},{16,0},{1,17},{17,1},{2,18},{18,2},{3,19},{19,3},{4,20},{20... | collective-permute-start | bytes 196616 | tf_op jit(solution)/shard_map/ppermute | solution.py:20
Sparse Core Ops, SparseCore 0:
  11.7 149.9 all-reduce.2
  168.5 129.4 all-reduce.4
where the time goes:
time: 376 us; the launch traced here: 375 us
  waiting for transfers between devices  284 us (76%)
  blocking collectives  30.8 us (8%)
  starting transfers between devices  24.5 us (7%)
  other arithmetic  16.6 us (4%)
  between operations  14.3 us (4%)
  local copies, waits for them, and re-layouts  4.94 us (1%)
    psum x1, waiting for transfers between devices, shards(): lax.psum(lax.cond(ffn_side, lambda: jnp.einsum('td,fd->tf', weighted, dow...  150 us
    psum x1, waiting for transfers between devices, shards(): lax.psum(lax.cond(ffn_side, product, lambda: jnp.zeros((total_rows, featu...  119 us
    psum x1, blocking collectives, row_statistic(): return lax.psum(partial_dot, 'dp')  30.8 us
    ppermute x4, starting transfers between devices, from_partner(): return lax.ppermute(value, axis, pairs)  23 us
    ppermute x4, waiting for transfers between devices, from_partner(): return lax.ppermute(value, axis, pairs)  15.1 us
  transfers between devices with their start and end apart: 7, of which 4 were waited for; matrix products, arithmetic and copies ran while one was open for 3% of the time, Pallas kernels for 0%

commit v1 on v0

--- a/solution.py
+++ b/solution.py
@@ -6,6 +6,12 @@
 D = 4096
 POS = 36
 LEN = 4096
+
+
+def gather_and_add(x, axis):
+    parts = lax.all_gather(x, axis, axis=0, tiled=False)
+    total = parts.sum(axis=0)
+    return total
 
 
 def shifted(value, axis, steps):
@@ -121,7 +127,7 @@
             "tf,df->td", up_delta, up_weight, preferred_element_type=jnp.float32
         )
 
-    normed_delta = lax.psum(
+    normed_delta = gather_and_add(
         lax.cond(ffn_side, product, lambda: jnp.zeros((total_rows, features), jnp.float32)).astype(
             jnp.bfloat16
         ),

time: 376 us -> 317 us (0.84)
  the two profiles are of different devices: /device:TPU:14 before, /device:TPU:2 now
where the time goes in v1:
time: 317 us; the launch traced here: 316 us
  waiting for transfers between devices  218 us (69%)
  blocking collectives  31.8 us (10%)
  starting transfers between devices  26 us (8%)
  other arithmetic  22 us (7%)
  between operations  14.3 us (5%)
    psum x1, waiting for transfers between devices, shards(): lax.psum(lax.cond(ffn_side, lambda: jnp.einsum('td,fd->tf', weighted, dow...  150 us
    all_gather x1, waiting for transfers between devices, gather_and_add(): parts = lax.all_gather(x, axis, axis=0, tiled=False)  53.5 us
    psum x1, blocking collectives, row_statistic(): return lax.psum(partial_dot, 'dp')  31.8 us
    ppermute x4, starting transfers between devices, from_partner(): return lax.ppermute(value, axis, pairs)  24.5 us
    ppermute x4, waiting for transfers between devices, from_partner(): return lax.ppermute(value, axis, pairs)  14.6 us
  transfers between devices with their start and end apart: 7, of which 4 were waited for; matrix products, arithmetic and copies ran while one was open for 4% of the time, Pallas kernels for 0%

profile of v1, /device:TPU:2, one launch (start us, length us, event | category | flops | bytes accessed | tf_op | source)
XLA Modules:
  0.0 316.1 jit_solution(14834627990252211231)
XLA Ops:
  7.2 0.7 divide_multiply_fusion
  7.9 0.1 select_reduce_fusion
  8.0 0.8 select_reduce_fusion.1
  8.8 1.3 multiply_convert_fusion
  10.1 0.2 conditional.5
  10.1 0.2 broadcast.64
  10.3 1.3 copy-done.2
  11.6 150.2 %all-reduce.2.cloned.1.call-done = bf16[1152,896]{1,0:T(8,128)(2,1)} async-done(((bf16[1152,896]{1,0:T(8,128)(2,1)}), bf16[1152,896]{1,0:T(8,128)(2,1)}) %all-reduce.2.cloned.1.call-update) | async-done | bytes 2064400 | tf_op jit(solution)/shard_map/psum | solution.py:102
  161.8 5.8 %fusion.3 = (bf16[1152,896]{1,0:T(8,128)(2,1)}, bf16[1152,896]{1,0:T(8,128)(2,1)S(1)}, bf16[1152,896]{1,0:T(8,128)(2,1)}) fusion(bf16[1152,896]{1,0:T(8,128)(2,1)} %param.28, bf16[1152,896]{1,0:T(8,128)(2,1)} %param.27, bf16[1152,896]{1,0:T(8,128)(2,1)} %all-reduce.2.cloned.1.call-done), kind=kLoop, calls=%fused_computation.10 | loop fusion | flops 19611648 | bytes 12386304 | tf_op jit(solution)/shard_map/convert_element_type | solution.py:94
  167.7 0.8 copy-done.3
  168.5 0.1 conditional.9
  168.6 10.1 %collective-permute-start.4 = (bf16[896,128]{1,0:T(8,128)(2,1)S(1)}, bf16[896,128]{1,0:T(8,128)(2,1)}, u32[]{:S(2)}, u32[]{:S(2)}) collective-permute-start(bf16[896,128]{1,0:T(8,128)(2,1)S(1)} %slice.39), channel_id=1, source_target_pairs={{0,16},{16,0},{1,17},{17,1},{2,18},{18,2},{3,19},{19,3},{4,20},{20... | collective-permute-start | bytes 688136 | tf_op jit(solution)/shard_map/ppermute | solution.py:26
  178.7 53.5 %all-gather.3.cloned.1.call-done = bf16[18432,256]{1,0:T(8,128)(2,1)} async-done(((bf16[1152,256]{1,0:T(8,128)(2,1)}), bf16[18432,256]{1,0:T(8,128)(2,1)}) %all-gather.3.cloned.1.call-update) | async-done | bytes 9437200 | tf_op jit(solution)/shard_map/all_gather | solution.py:12
  232.3 5.4 %reduce_sum.41 = bf16[1152,256]{1,0:T(8,128)(2,1)S(1)} reduce(bf16[16,1152,256]{2,1,0:T(8,128)(2,1)} %bitcast.15, bf16[]{:T(256)} %constant.56.clone.1), dimensions={0}, to_apply=%region_7.8 | reduce | flops 4423680 | bytes 10027010 | tf_op jit(solution)/shard_map/reduce_sum | solution.py:13
  237.7 1.3 fusion.13
  239.0 31.8 %psum.15 = f32[1152]{0:T(1024)S(1)} all-reduce(f32[1152]{0:T(1024)S(1)} %fusion.13), channel_id=1, replica_groups=mesh['dp'=16,'segment'=2,'tensor'=16] {'dp'}, use_global_device_ids=true, to_apply=%region_9.10 | all-reduce | flops 1152 | bytes 9216 | tf_op jit(solution)/shard_map/psum | solution.py:50
  270.8 2.7 fusion.15
  273.5 0.1 conditional.8
  273.6 6.6 %collective-permute-start.3 = (bf16[128,896]{1,0:T(8,128)(2,1)S(1)}, bf16[128,896]{1,0:T(8,128)(2,1)S(1)}, u32[]{:S(2)}, u32[]{:S(2)}) collective-permute-start(bf16[128,896]{1,0:T(8,128)(2,1)S(1)} %slice.37), channel_id=1, source_target_pairs={{0,16},{16,0},{1,17},{17,1},{2,18},{18,2},{3,19},{19,3},{4,20},{20... | collective-permute-start | bytes 688136 | tf_op jit(solution)/shard_map/ppermute | solution.py:26
  280.2 1.4 collective-permute-start
  281.7 1.8 slice_select_fusion
  283.5 6.0 %collective-permute-start.2 = (bf16[128,896]{1,0:T(8,128)(2,1)S(1)}, bf16[128,896]{1,0:T(8,128)(2,1)S(1)}, u32[]{:S(2)}, u32[]{:S(2)}) collective-permute-start(bf16[128,896]{1,0:T(8,128)(2,1)S(1)} %slice.35), channel_id=1, source_target_pairs={{0,16},{16,0},{1,17},{17,1},{2,18},{18,2},{3,19},{19,3},{4,20},{20... | collective-permute-start | bytes 688136 | tf_op jit(solution)/shard_map/ppermute | solution.py:26
  289.5 0.7 slice_select_fusion.1
  290.2 9.5 %collective-permute-done.2 = bf16[128,896]{1,0:T(8,128)(2,1)S(1)} collective-permute-done((bf16[128,896]{1,0:T(8,128)(2,1)S(1)}, bf16[128,896]{1,0:T(8,128)(2,1)S(1)}, u32[]{:S(2)}, u32[]{:S(2)}) %collective-permute-start.2) | collective-permute-done | bytes 229408 | tf_op jit(solution)/shard_map/ppermute | solution.py:26
  299.7 0.7 slice_select_fusion.2
  300.4 0.1 broadcast_select_fusion
  300.5 0.4 conditional.7
  300.5 0.4 fusion.27
  300.9 1.9 collective-permute-start.1
  302.9 0.6 constant_dynamic-slice_fusion
  303.5 5.1 %collective-permute-done.1 = bf16[256,128]{1,0:T(8,128)(2,1)S(1)} collective-permute-done((bf16[256,128]{1,0:T(8,128)(2,1)S(1)}, bf16[256,128]{1,0:T(8,128)(2,1)S(1)}, u32[]{:S(2)}, u32[]{:S(2)}) %collective-permute-start.1) | collective-permute-done | bytes 65568 | tf_op jit(solution)/shard_map/ppermute | solution.py:26
  308.6 0.6 slice_select_fusion.3
  (35 shorter events, 0.4 us)
Async XLA Ops:
  7.2 154.7 %all-reduce.2.cloned.1.call-start = ((), (), s32[]{:S(2)}) async-start(), calls=%async_computation | async-start | bytes 4128768 | tf_op jit(solution)/shard_map/psum | solution.py:102
  10.3 1.3 copy-start.2
  11.6 220.7 %all-gather.3.cloned.1.call-start = ((), (), s32[]{:S(2)}) async-start(), calls=%async_computation.1 | async-start | bytes 10027008 | tf_op jit(solution)/shard_map/all_gather | solution.py:12
  167.7 0.8 copy-start.3
  168.6 63.6 %copy-start.6 = (bf16[896,256]{1,0:T(8,128)(2,1)}, bf16[896,256]{1,0:T(8,128)(2,1)S(1)}, u32[]{:S(2)}) copy-start(bf16[896,256]{1,0:T(8,128)(2,1)S(1)} %get-tuple-element.80) | copy-start | bytes 1376260
  168.6 113.0 %collective-permute-start.4 = (bf16[896,128]{1,0:T(8,128)(2,1)S(1)}, bf16[896,128]{1,0:T(8,128)(2,1)}, u32[]{:S(2)}, u32[]{:S(2)}) collective-permute-start(bf16[896,128]{1,0:T(8,128)(2,1)S(1)} %slice.39), channel_id=1, source_target_pairs={{0,16},{16,0},{1,17},{17,1},{2,18},{18,2},{3,19},{19,3},{4,20},{20... | collective-permute-start | bytes 688136 | tf_op jit(solution)/shard_map/ppermute | solution.py:26
  232.3 5.4 %copy-start.9 = (f32[256]{0:T(256)S(1)}, f32[256]{0:T(256)}, u32[]{:S(2)}) copy-start(f32[256]{0:T(256)} %param.26) | copy-start | bytes 3076
  232.3 38.5 %copy-start.8 = (f32[1152]{0:T(1024)S(1)}, f32[1152]{0:T(1024)}, u32[]{:S(2)}) copy-start(f32[1152]{0:T(1024)} %param.25) | copy-start | bytes 13828
  232.3 38.6 %copy-start.4 = (bf16[1152,256]{1,0:T(8,128)(2,1)S(1)}, bf16[1152,256]{1,0:T(8,128)(2,1)}, u32[]{:S(2)}) copy-start(bf16[1152,256]{1,0:T(8,128)(2,1)} %param.29) | copy-start | bytes 1769476
  270.8 2.7 copy-start
  273.5 6.7 %copy-start.5 = (bf16[1152,256]{1,0:T(8,128)(2,1)S(1)}, bf16[1152,256]{1,0:T(8,128)(2,1)}, u32[]{:S(2)}) copy-start(bf16[1152,256]{1,0:T(8,128)(2,1)} %get-tuple-element.72) | copy-start | bytes 1769476
  273.6 15.8 %collective-permute-start.3 = (bf16[128,896]{1,0:T(8,128)(2,1)S(1)}, bf16[128,896]{1,0:T(8,128)(2,1)S(1)}, u32[]{:S(2)}, u32[]{:S(2)}) collective-permute-start(bf16[128,896]{1,0:T(8,128)(2,1)S(1)} %slice.37), channel_id=1, source_target_pairs={{0,16},{16,0},{1,17},{17,1},{2,18},{18,2},{3,19},{19,3},{4,20},{20... | collective-permute-start | bytes 688136 | tf_op jit(solution)/shard_map/ppermute | solution.py:26
  280.2 20.3 %copy-start.10 = (bf16[1152,256]{1,0:T(8,128)(2,1)S(1)}, bf16[1152,256]{1,0:T(8,128)(2,1)}, u32[]{:S(2)}) copy-start(bf16[1152,256]{1,0:T(8,128)(2,1)} %param.23) | copy-start | bytes 1769476
  280.2 20.2 %collective-permute-start = (bf16[1152,256]{1,0:T(8,128)(2,1)S(1)}, bf16[1152,256]{1,0:T(8,128)(2,1)S(1)}, u32[]{:S(2)}, u32[]{:S(2)}) collective-permute-start(bf16[1152,256]{1,0:T(8,128)(2,1)S(1)} %copy-done.5), channel_id=1, source_target_pairs={{16,0},{17,1},{18,2},{19,3},{20,4},{21,5},{22,6},{23,7},{24,8},{25... | collective-permute-start | bytes 1769480 | tf_op jit(solution)/shard_map/ppermute | solution.py:20
  283.5 16.2 %collective-permute-start.2 = (bf16[128,896]{1,0:T(8,128)(2,1)S(1)}, bf16[128,896]{1,0:T(8,128)(2,1)S(1)}, u32[]{:S(2)}, u32[]{:S(2)}) collective-permute-start(bf16[128,896]{1,0:T(8,128)(2,1)S(1)} %slice.35), channel_id=1, source_target_pairs={{0,16},{16,0},{1,17},{17,1},{2,18},{18,2},{3,19},{19,3},{4,20},{20... | collective-permute-start | bytes 688136 | tf_op jit(solution)/shard_map/ppermute | solution.py:26
  300.9 7.7 %collective-permute-start.1 = (bf16[256,128]{1,0:T(8,128)(2,1)S(1)}, bf16[256,128]{1,0:T(8,128)(2,1)S(1)}, u32[]{:S(2)}, u32[]{:S(2)}) collective-permute-start(bf16[256,128]{1,0:T(8,128)(2,1)S(1)} %slice.32), channel_id=1, source_target_pairs={{0,16},{16,0},{1,17},{17,1},{2,18},{18,2},{3,19},{19,3},{4,20},{20... | collective-permute-start | bytes 196616 | tf_op jit(solution)/shard_map/ppermute | solution.py:26
Sparse Core Ops, SparseCore 0:
  11.7 150.0 all-reduce.1
  168.7 63.5 all-gather.2
